TPU v7x, 32 devices: a whole 2x2x4 slice. The times are simulated.
32 devices in a mesh: row: 4 (over z), col: 8 (over y, x, core).
Axes of the slice: x: 2, y: 2, z: 4, core: 2. Of those that a mesh axis runs over, the one named last changes fastest.
Arguments:
- trailing: float32 [16384, 3072], P('row', 'col'), may hold values from -6 to 6
- leaf_vectors: float32 [16384, 256], P(('row', 'col')), may hold values from -1 to 1, as said below
- leaf_factor: float32 [1024, 256], P(('row', 'col')), may hold values from -1 to 2, as said below
- tree_vectors: float32 [1024, 256], P(('row', 'col')), may hold values from -1 to 1, as said below
- tree_factor: float32 [1024, 256], P(('row', 'col')), may hold values from -1 to 2, as said below
Outputs:
- updated: float32 [16384, 3072], P('row', 'col')
Inputs may be any that keep to these rules, and one draw needn't show every extreme that they name: `leaf_vectors`: in each row block of 4096 rows, row r < 256 of the block holds 1 in column r and 0 in every column after r. `leaf_factor`: each 256 x 256 block is upper triangular with its diagonal between 1 and 2. `tree_vectors`: each 256 x 256 block is upper triangular. `tree_factor`: each 256 x 256 block is upper triangular with its diagonal between 1 and 2.
All inputs are finite; a program needn't handle non-finite values.
Results may differ from a plain program's by a relative error of at most 0.0002.
Values sent between devices are 32-bit elements; how exact they have to be, the bound alone decides.
No kernel may reach another device: no remote copies, remote signals or barrier semaphores. Data moves between devices by JAX's collectives and lax.ppermute only.
A program may use at most 128 MiB of HBM per device.

v0:
```python
import jax
import jax.numpy as jnp
from jax import lax
from jax.sharding import PartitionSpec as P

highest = lax.Precision.HIGHEST
contract_rows = (((0,), (0,)), ((), ()))


def swapped(array, axis, apart):
    return lax.ppermute(array, axis, [(i, i ^ 1 << apart) for i in range(lax.axis_size(axis))])


def left_product(first, second):
    return lax.dot_general(
        first, second, contract_rows, precision=highest, preferred_element_type=jnp.float32
    )


def plain_product(first, second):
    return jnp.dot(first, second, precision=highest, preferred_element_type=jnp.float32)


def shards(trailing, leaf_vectors, leaf_factor, tree_vectors, tree_factor):
    panel_width = leaf_factor.shape[1]
    panel, block_factor, own_vectors, own_factor = (
        lax.all_gather(leaf_vectors, "col", axis=0, tiled=True),
        lax.all_gather(leaf_factor, "col", axis=0, tiled=True),
        lax.all_gather(tree_vectors, "col", axis=0, tiled=True),
        lax.all_gather(tree_factor, "col", axis=0, tiled=True),
    )
    weights = left_product(block_factor, left_product(panel, trailing))
    updated = trailing - plain_product(panel, weights)
    upper_rows = updated[:panel_width]
    lower_rows = updated[panel_width:]
    sections = lax.axis_size("row").bit_length() - 1
    position = lax.axis_index("row")
    pair_vectors, pair_factor = (
        lax.all_gather(own_vectors, "row", axis=0, tiled=True),
        lax.all_gather(own_factor, "row", axis=0, tiled=True),
    )
    current = upper_rows
    final_top = upper_rows
    for level_bit in range(sections):
        stride = 1 << level_bit
        partner_top = swapped(current, "row", level_bit)
        on_upper = position // stride % 2 == 1
        lower_group = jnp.where(on_upper, partner_top, current)
        upper_group = jnp.where(on_upper, current, partner_top)
        chosen = position // (2 * stride) * (2 * stride) + stride
        vectors = lax.dynamic_slice_in_dim(pair_vectors, chosen * panel_width, panel_width, 0)
        factor = lax.dynamic_slice_in_dim(pair_factor, chosen * panel_width, panel_width, 0)
        tree_weights = left_product(factor, lower_group + left_product(vectors, upper_group))
        final_top = jnp.where(
            position % (2 * stride) == stride,
            upper_group - plain_product(vectors, tree_weights),
            final_top,
        )
        current = lower_group - tree_weights
    final_top = jnp.where(position == 0, current, final_top)
    return jnp.concatenate([final_top, lower_rows], 0)


def solution(mesh):
    placed = (
        P("row", "col"),
        P(("row", "col"), None),
        P(("row", "col"), None),
        P(("row", "col"), None),
        P(("row", "col"), None),
    )
    return jax.shard_map(
        shards, mesh=mesh, in_specs=placed, out_specs=P("row", "col"), check_vma=False
    )
```

profile of v0, /device:TPU:0, one launch (start us, length us, event | category | flops | bytes accessed | tf_op | source)
XLA Modules:
  0.0 161.5 jit_solution(10669404419144354708)
XLA Ops:
  6.5 0.0 all-gather.4.cloned.1.call-start
  6.5 0.7 all-gather.4.cloned.1.call-update
  7.3 0.0 all-gather.8.cloned.1.call-start
  7.3 12.6 %all_gather.22 = f32[256,256]{1,0:T(8,128)} all-gather(f32[32,256]{1,0:T(8,128)} %param.8), channel_id=1, replica_groups=mesh['row'=4,'col'=8] {'col'}, dimensions={0}, use_global_device_ids=true | all-gather | bytes 294912 | tf_op jit(solution)/shard_map/all_gather | solution.py:29
  19.9 0.0 all-gather.8.cloned.1.call-update
  19.9 0.0 all-gather.6.cloned.1.call-start
  20.0 10.6 %all_gather.20 = f32[256,256]{1,0:T(8,128)} all-gather(f32[32,256]{1,0:T(8,128)} %param.9), channel_id=1, replica_groups=mesh['row'=4,'col'=8] {'col'}, dimensions={0}, use_global_device_ids=true | all-gather | bytes 294912 | tf_op jit(solution)/shard_map/all_gather | solution.py:30
  30.6 0.0 all-gather.6.cloned.1.call-update
  30.6 9.8 %all_gather.19 = f32[256,256]{1,0:T(8,128)S(1)} all-gather(f32[32,256]{1,0:T(8,128)} %param.7), channel_id=1, replica_groups=mesh['row'=4,'col'=8] {'col'}, dimensions={0}, use_global_device_ids=true | all-gather | bytes 294912 | tf_op jit(solution)/shard_map/all_gather | solution.py:28
  40.4 6.6 %copy.6 = f32[4096,384]{0,1:T(8,128)} copy(f32[4096,384]{1,0:T(8,128)} %param.5) | data formatting | bytes 12582912 | tf_op args[0]
  47.0 3.2 %all-gather.4.cloned.1.call-done = f32[4096,256]{1,0:T(8,128)} async-done(((f32[512,256]{1,0:T(8,128)}), f32[4096,256]{1,0:T(8,128)}) %all-gather.4.cloned.1.call-update) | async-done | bytes 4194320 | tf_op jit(solution)/shard_map/all_gather | solution.py:27
  50.2 0.0 copy-start.1
  50.2 0.0 copy-start.2
  50.2 9.9 %fusion.20 = f32[256,384]{1,0:T(8,128)S(1)} fusion(f32[4096,256]{1,0:T(8,128)} %all-gather.4.cloned.1.call-done, f32[4096,384]{1,0:T(8,128)} %param.5), kind=kOutput, calls=%fused_computation.29 | convolution fusion | flops 4831838208 | bytes 10878976 | tf_op jit(solution)/shard_map/dot_general | solution.py:15
  60.2 0.8 fusion.21
  61.0 0.0 copy-done.1
  61.0 0.0 copy-done.2
  61.0 6.0 %bitcast_subtract_fusion = f32[4096,384]{0,1:T(8,128)S(1)} fusion(f32[4096,384]{0,1:T(8,128)S(1)} %copy-done.1, f32[384,256]{1,0:T(8,128)S(1)} %fusion.21, f32[4096,256]{1,0:T(8,128)S(1)} %copy-done.2), kind=kOutput, calls=%fused_computation.1 | convolution fusion | flops 4833411072 | bytes 17170432 | tf_op jit(solution)/shard_map/dot_general | solution.py:21
  67.0 0.0 copy-start
  67.0 2.7 %copy-done = f32[4096,384]{0,1:T(8,128)} copy-done((f32[4096,384]{0,1:T(8,128)}, f32[4096,384]{0,1:T(8,128)S(1)}, u32[]{:S(2)}) %copy-start) | copy-done | bytes 6291480
  69.8 1.5 collective-permute-start
  71.3 10.8 %all-gather.8.cloned.1.call-done = f32[1024,256]{1,0:T(8,128)} async-done(((f32[256,256]{1,0:T(8,128)}), f32[1024,256]{1,0:T(8,128)}) %all-gather.8.cloned.1.call-update) | async-done | bytes 1048592 | tf_op jit(solution)/shard_map/all_gather | solution.py:39
  82.1 5.2 %collective-permute-done = f32[256,384]{0,1:T(8,128)S(1)} collective-permute-done((f32[256,384]{0,1:T(8,128)S(1)}, f32[256,384]{0,1:T(8,128)S(1)}, u32[]{:S(2)}, u32[]{:S(2)}) %collective-permute-start) | collective-permute-done | bytes 393248 | tf_op jit(solution)/shard_map/ppermute | solution.py:11
  87.3 1.7 %convolution_add_fusion.1 = f32[256,384]{0,1:T(8,128)S(1)} fusion(f32[1024,256]{1,0:T(8,128)} %all-gather.8.cloned.1.call-done, s32[]{:T(128)S(6)} %select_n.79, f32[256,384]{0,1:T(8,128)S(1)} %collective-permute-done, pred[]{:T(512)S(6)} %eq.20, f32[4096,384]{0,1:T(8,128)} %copy-done), kind=kOutput, calls=%fused_computation.7 | convolution fusion | flops 302284800 | bytes 2229760 | tf_op jit(solution)/shard_map/dot_general | solution.py:15
  89.0 26.9 %all-gather.6.cloned.1.call-done = f32[1024,256]{1,0:T(8,128)} async-done(((f32[256,256]{1,0:T(8,128)}), f32[1024,256]{1,0:T(8,128)}) %all-gather.6.cloned.1.call-update) | async-done | bytes 1048592 | tf_op jit(solution)/shard_map/all_gather | solution.py:40
  115.9 2.0 %fusion.4 = f32[256,384]{1,0:T(8,128)S(1)} fusion(f32[256,384]{0,1:T(8,128)S(1)} %convolution_add_fusion.1, f32[1024,256]{1,0:T(8,128)} %all-gather.6.cloned.1.call-done, s32[]{:T(128)S(6)} %select_n.79), kind=kOutput, calls=%fused_computation.11 | convolution fusion | flops 301989888 | bytes 1048580 | tf_op jit(solution)/shard_map/dot_general | solution.py:15
  117.9 0.2 copy.7
  118.0 1.1 fusion.12
  119.1 0.0 copy-start.3
  119.1 1.9 %collective-permute-start.1 = (f32[256,384]{0,1:T(8,128)S(1)}, f32[256,384]{0,1:T(8,128)S(1)}, u32[]{:S(2)}, u32[]{:S(2)}) collective-permute-start(f32[256,384]{0,1:T(8,128)S(1)} %fusion.12), channel_id=1, source_target_pairs={{0,16},{8,24},{16,0},{24,8},{1,17},{9,25},{17,1},{25,9},{2,18},{10... | collective-permute-start | bytes 1179656 | tf_op jit(solution)/shard_map/ppermute | solution.py:11
  121.0 5.6 %slice.9 = f32[3840,384]{0,1:T(8,128)} slice(f32[4096,384]{0,1:T(8,128)} %copy-done), slice={[256:4096], [0:384]} | slice | bytes 11796480 | tf_op jit(solution)/shard_map/slice | solution.py:35
  126.6 0.0 copy-done.3
  126.6 1.8 %fusion = f32[256,384]{0,1:T(8,128)S(1)} fusion(f32[256,384]{1,0:T(8,128)S(1)} %fusion.4, f32[1024,256]{1,0:T(8,128)S(1)} %copy-done.3, s32[]{:T(128)S(6)} %select_n.79, pred[]{:T(512)S(6)} %eq.20, f32[256,384]{0,1:T(8,128)S(1)} %collective-permute-done, f32[4096,384]{0,1:T(8,128)} %copy-done), kind=kOutput, calls=%fused_computation.3 | convolution fusion | flops 302284800 | bytes 1835013 | tf_op jit(solution)/shard_map/dot_general | solution.py:21
  128.4 10.5 %collective-permute-done.1 = f32[256,384]{0,1:T(8,128)S(1)} collective-permute-done((f32[256,384]{0,1:T(8,128)S(1)}, f32[256,384]{0,1:T(8,128)S(1)}, u32[]{:S(2)}, u32[]{:S(2)}) %collective-permute-start.1) | collective-permute-done | bytes 393248 | tf_op jit(solution)/shard_map/ppermute | solution.py:11
  138.9 0.5 convolution_add_fusion
  139.4 2.0 %fusion.2 = f32[256,384]{1,0:T(8,128)S(1)} fusion(f32[256,384]{0,1:T(8,128)S(1)} %convolution_add_fusion, f32[1024,256]{1,0:T(8,128)} %all-gather.6.cloned.1.call-done, s32[]{:T(128)S(6)} %select_n.83), kind=kOutput, calls=%fused_computation.9 | convolution fusion | flops 301989888 | bytes 1048580 | tf_op jit(solution)/shard_map/dot_general | solution.py:15
  141.4 0.2 copy.8
  141.6 0.8 subtract_select_fusion
  142.4 6.0 %pad_maximum_fusion = f32[4096,384]{0,1:T(8,128)} fusion(f32[3840,384]{0,1:T(8,128)} %slice.9, f32[256,384]{0,1:T(8,128)S(1)} %subtract_select_fusion), kind=kLoop, calls=%fused_computation | loop fusion | flops 1572864 | bytes 12582912 | tf_op jit(solution)/shard_map/concatenate | solution.py:61
  148.5 6.6 %copy.11 = f32[4096,384]{1,0:T(8,128)} copy(f32[4096,384]{0,1:T(8,128)} %pad_maximum_fusion) | data formatting | bytes 12582912 | tf_op jit(solution)/shard_map/concatenate | solution.py:61
  (1 shorter events, 0.0 us)
Async XLA Ops:
  6.5 43.7 %all-gather.4.cloned.1.call-start = ((), (), s32[]{:S(2)}) async-start(), calls=%async_computation | async-start | bytes 4718592 | tf_op jit(solution)/shard_map/all_gather | solution.py:27
  7.3 74.9 %all-gather.8.cloned.1.call-start = ((), (), s32[]{:S(2)}) async-start(), calls=%async_computation.2 | async-start | bytes 1310720 | tf_op jit(solution)/shard_map/all_gather | solution.py:39
  19.9 96.0 %all-gather.6.cloned.1.call-start = ((), (), s32[]{:S(2)}) async-start(), calls=%async_computation.1 | async-start | bytes 1310720 | tf_op jit(solution)/shard_map/all_gather | solution.py:40
  50.2 10.7 %copy-start.1 = (f32[4096,384]{0,1:T(8,128)S(1)}, f32[4096,384]{0,1:T(8,128)}, u32[]{:S(2)}) copy-start(f32[4096,384]{0,1:T(8,128)} %copy.6) | copy-start | bytes 18874372
  50.2 10.7 %copy-start.2 = (f32[4096,256]{1,0:T(8,128)S(1)}, f32[4096,256]{1,0:T(8,128)}, u32[]{:S(2)}) copy-start(f32[4096,256]{1,0:T(8,128)} %all-gather.4.cloned.1.call-done) | copy-start | bytes 12582916
  67.0 2.7 %copy-start = (f32[4096,384]{0,1:T(8,128)}, f32[4096,384]{0,1:T(8,128)S(1)}, u32[]{:S(2)}) copy-start(f32[4096,384]{0,1:T(8,128)S(1)} %bitcast_subtract_fusion) | copy-start | bytes 18874372
  69.8 17.5 %collective-permute-start = (f32[256,384]{0,1:T(8,128)S(1)}, f32[256,384]{0,1:T(8,128)S(1)}, u32[]{:S(2)}, u32[]{:S(2)}) collective-permute-start(f32[256,384]{0,1:T(8,128)S(1)} %slice.8), channel_id=1, source_target_pairs={{0,8},{8,0},{16,24},{24,16},{1,9},{9,1},{17,25},{25,17},{2,10},{10... | collective-permute-start | bytes 1179656 | tf_op jit(solution)/shard_map/ppermute | solution.py:11
  119.1 7.4 %copy-start.3 = (f32[1024,256]{1,0:T(8,128)S(1)}, f32[1024,256]{1,0:T(8,128)}, u32[]{:S(2)}) copy-start(f32[1024,256]{1,0:T(8,128)} %all-gather.8.cloned.1.call-done) | copy-start | bytes 3145732
  119.1 19.8 %collective-permute-start.1 = (f32[256,384]{0,1:T(8,128)S(1)}, f32[256,384]{0,1:T(8,128)S(1)}, u32[]{:S(2)}, u32[]{:S(2)}) collective-permute-start(f32[256,384]{0,1:T(8,128)S(1)} %fusion.12), channel_id=1, source_target_pairs={{0,16},{8,24},{16,0},{24,8},{1,17},{9,25},{17,1},{25,9},{2,18},{10... | collective-permute-start | bytes 1179656 | tf_op jit(solution)/shard_map/ppermute | solution.py:11
Sparse Core Ops, SparseCore 0:
  9.2 40.9 all-gather.3
  51.8 30.2 all-gather.7
  83.7 32.1 all-gather.5
where the time goes:
time: 162 us
  waiting for transfers between devices  57.4 us (35%)
  blocking collectives  33 us (20%)
  matrix products  25.5 us (16%)
  local copies, waits for them, and re-layouts  21.8 us (13%)
  between operations  13.2 us (8%)
  other arithmetic  7.11 us (4%)
  starting transfers between devices  3.49 us (2%)
    all_gather x1, waiting for transfers between devices, shards(): lax.all_gather(own_factor, 'row', axis=0, tiled=True)  26.9 us
    dot_general x6, matrix products, left_product(): lax.dot_general(first, second, contract_rows, precision=highest, preferre...  16.9 us
    ppermute x2, waiting for transfers between devices, swapped(): lax.ppermute(array, axis, [(i, i ^ 1 << apart) for i in range(lax.axis_si...  15.7 us
    all_gather x1, blocking collectives, shards(): lax.all_gather(tree_vectors, 'col', axis=0, tiled=True)  12.6 us
    all_gather x1, waiting for transfers between devices, shards(): lax.all_gather(own_vectors, 'row', axis=0, tiled=True)  10.8 us
    all_gather x1, blocking collectives, shards(): lax.all_gather(tree_factor, 'col', axis=0, tiled=True)  10.6 us
    all_gather x1, blocking collectives, shards(): lax.all_gather(leaf_factor, 'col', axis=0, tiled=True)  9.82 us
    unnamed x9, local copies, waits for them, and re-layouts  9.34 us
  transfers between devices with their start and end apart: 5, of which 5 were waited for; matrix products, arithmetic and copies ran while one was open for 20% of the time, Pallas kernels for 0%

commit v1 on v0

--- a/solution.py
+++ b/solution.py
@@ -5,6 +5,28 @@
 
 highest = lax.Precision.HIGHEST
 contract_rows = (((0,), (0,)), ((), ()))
+
+
+def joined_along(blocks, dim):
+    dims = list(blocks.shape[1:])
+    dims[dim] *= blocks.shape[0]
+    return jnp.moveaxis(blocks, 0, dim).reshape(dims)
+
+
+def gather_around(shard, axis, dim):
+    peers = lax.axis_size(axis)
+    pairs = [(i, (i + 1) % peers) for i in range(peers)]
+    back = [(b, a) for a, b in pairs]
+    lower, upper = ([], [])
+    for step in range(peers - 1):
+        if step % 2 == 0:
+            lower.append(lax.ppermute(lower[-1] if lower else shard, axis, pairs))
+        else:
+            upper.append(lax.ppermute(upper[-1] if upper else shard, axis, back))
+    blocks = jnp.stack([*lower[::-1], shard, *upper])
+    shift = lax.axis_index(axis) - len(lower)
+    blocks = blocks[(jnp.arange(peers) - shift) % peers]
+    return joined_along(blocks, dim)
 
 
 def swapped(array, axis, apart):
@@ -37,7 +59,7 @@
     position = lax.axis_index("row")
     pair_vectors, pair_factor = (
         lax.all_gather(own_vectors, "row", axis=0, tiled=True),
-        lax.all_gather(own_factor, "row", axis=0, tiled=True),
+        gather_around(own_factor, "row", 0),
     )
     current = upper_rows
     final_top = upper_rows

time: 162 us -> 135 us (0.83)
  waiting for transfers between devices: 57.4 us -> 26.7 us
  starting transfers between devices: 3.49 us -> 8.48 us
    all_gather x1 -> x0, waiting for transfers between devices: 26.9 us -> none  [shards(): lax.all_gather(own_factor, 'row', axis=0, tiled=True)]
    ppermute x0 -> x3, starting transfers between devices: none -> 4.42 us  [the longest x1 2.25 us: gather_around(): upper.append(lax.ppermute(upper[-1] if upper else shard, axis, back))]
    all_gather x1, waiting for transfers between devices: 3.21 us -> 0.45 us  [shards(): lax.all_gather(leaf_vectors, 'col', axis=0, tiled=True)]
    all_gather x1, blocking collectives: 12.6 us -> 10.6 us  [shards(): lax.all_gather(tree_vectors, 'col', axis=0, tiled=True)]
    dot_general x6, matrix products: 16.9 us -> 15 us  [left_product(): lax.dot_general(first, second, contract_rows, precision=highest, preferre...]
    unnamed x9 -> x11, local copies, waits for them, and re-layouts: 9.34 us -> 9.33 us
  transfers between devices with their start and end apart: 5 -> 7, of which waited for: 5 -> 4; matrix products, arithmetic and copies ran while one was open for 20% -> 23% of each run, Pallas kernels for 0% -> 0%
where the time goes in v1:
time: 135 us
  blocking collectives  31.5 us (23%)
  waiting for transfers between devices  26.7 us (20%)
  matrix products  24.6 us (18%)
  local copies, waits for them, and re-layouts  22.5 us (17%)
  between operations  13.6 us (10%)
  starting transfers between devices  8.48 us (6%)
  other arithmetic  7.22 us (5%)
    ppermute x2, waiting for transfers between devices, swapped(): lax.ppermute(array, axis, [(i, i ^ 1 << apart) for i in range(lax.axis_si...  15.5 us
    dot_general x6, matrix products, left_product(): lax.dot_general(first, second, contract_rows, precision=highest, preferre...  15 us
    all_gather x1, blocking collectives, shards(): lax.all_gather(tree_factor, 'col', axis=0, tiled=True)  11 us
    all_gather x1, blocking collectives, shards(): lax.all_gather(tree_vectors, 'col', axis=0, tiled=True)  10.6 us
    all_gather x1, waiting for transfers between devices, shards(): lax.all_gather(own_vectors, 'row', axis=0, tiled=True)  10.1 us
    all_gather x1, blocking collectives, shards(): lax.all_gather(leaf_factor, 'col', axis=0, tiled=True)  9.9 us
    dot_general x3, matrix products, plain_product(): jnp.dot(first, second, precision=highest, preferred_element_type=jnp.floa...  9.59 us
    unnamed x11, local copies, waits for them, and re-layouts  9.33 us
  transfers between devices with their start and end apart: 7, of which 4 were waited for; matrix products, arithmetic and copies ran while one was open for 23% of the time, Pallas kernels for 0%

profile of v1, /device:TPU:0, one launch (start us, length us, event | category | flops | bytes accessed | tf_op | source)
XLA Modules:
  0.0 134.6 jit_solution(289919218524241334)
XLA Ops:
  6.5 0.0 all-gather.3.cloned.1.call-start
  6.5 0.7 all-gather.3.cloned.1.call-update
  7.3 0.0 all-gather.5.cloned.1.call-start
  7.3 11.0 %all_gather.17 = f32[256,256]{1,0:T(8,128)S(1)} all-gather(f32[32,256]{1,0:T(8,128)} %param.9), channel_id=1, replica_groups=mesh['row'=4,'col'=8] {'col'}, dimensions={0}, use_global_device_ids=true | all-gather | bytes 294912 | tf_op jit(solution)/shard_map/all_gather | solution.py:52
  18.3 1.6 %collective-permute-start.1 = (f32[256,256]{1,0:T(8,128)S(1)}, f32[256,256]{1,0:T(8,128)S(1)}, u32[]{:S(2)}, u32[]{:S(2)}) collective-permute-start(f32[256,256]{1,0:T(8,128)S(1)} %all_gather.17), channel_id=1, source_target_pairs={{0,8},{8,16},{16,24},{24,0},{1,9},{9,17},{17,25},{25,1},{2,10},{10... | collective-permute-start | bytes 786440 | tf_op jit(solution)/shard_map/ppermute | solution.py:23
  19.9 2.2 %collective-permute-start.3 = (f32[256,256]{1,0:T(8,128)S(1)}, f32[256,256]{1,0:T(8,128)S(1)}, u32[]{:S(2)}, u32[]{:S(2)}) collective-permute-start(f32[256,256]{1,0:T(8,128)S(1)} %all_gather.17), channel_id=1, source_target_pairs={{8,0},{16,8},{24,16},{0,24},{9,1},{17,9},{25,17},{1,25},{10,2},{18... | collective-permute-start | bytes 786440 | tf_op jit(solution)/shard_map/ppermute | solution.py:25
  22.1 10.6 %all_gather.18 = f32[256,256]{1,0:T(8,128)} all-gather(f32[32,256]{1,0:T(8,128)} %param.8), channel_id=1, replica_groups=mesh['row'=4,'col'=8] {'col'}, dimensions={0}, use_global_device_ids=true | all-gather | bytes 294912 | tf_op jit(solution)/shard_map/all_gather | solution.py:51
  32.7 0.0 all-gather.5.cloned.1.call-update
  32.7 0.0 copy-start.4
  32.7 6.6 %copy.6 = f32[4096,384]{0,1:T(8,128)} copy(f32[4096,384]{1,0:T(8,128)} %param.5) | data formatting | bytes 12582912 | tf_op args[0]
  39.4 0.0 copy-done.4
  39.4 9.9 %all_gather.16 = f32[256,256]{1,0:T(8,128)S(1)} all-gather(f32[32,256]{1,0:T(8,128)S(1)} %copy-done.4), channel_id=1, replica_groups=mesh['row'=4,'col'=8] {'col'}, dimensions={0}, use_global_device_ids=true | all-gather | bytes 294912 | tf_op jit(solution)/shard_map/all_gather | solution.py:50
  49.3 0.0 collective-permute-done.1
  49.3 0.6 collective-permute-start.2
  49.9 0.5 all-gather.3.cloned.1.call-done
  50.3 0.0 copy-start.1
  50.3 0.0 copy-start.2
  50.3 9.9 %fusion.22 = f32[256,384]{1,0:T(8,128)S(1)} fusion(f32[4096,256]{1,0:T(8,128)} %all-gather.3.cloned.1.call-done, f32[4096,384]{1,0:T(8,128)} %param.5), kind=kOutput, calls=%fused_computation.38 | convolution fusion | flops 4831838208 | bytes 10878976 | tf_op jit(solution)/shard_map/dot_general | solution.py:37
  60.2 0.8 fusion.23
  61.0 0.0 copy-done.1
  61.1 0.0 copy-done.2
  61.1 6.0 %bitcast_subtract_fusion = f32[4096,384]{0,1:T(8,128)S(1)} fusion(f32[4096,384]{0,1:T(8,128)S(1)} %copy-done.1, f32[384,256]{1,0:T(8,128)S(1)} %fusion.23, f32[4096,256]{1,0:T(8,128)S(1)} %copy-done.2), kind=kOutput, calls=%fused_computation.2 | convolution fusion | flops 4833411072 | bytes 17170432 | tf_op jit(solution)/shard_map/dot_general | solution.py:43
  67.1 0.0 copy-start
  67.1 2.7 %copy-done = f32[4096,384]{0,1:T(8,128)} copy-done((f32[4096,384]{0,1:T(8,128)}, f32[4096,384]{0,1:T(8,128)S(1)}, u32[]{:S(2)}) %copy-start) | copy-done | bytes 6291480
  69.8 1.6 %collective-permute-start = (f32[256,384]{0,1:T(8,128)S(1)}, f32[256,384]{0,1:T(8,128)S(1)}, u32[]{:S(2)}, u32[]{:S(2)}) collective-permute-start(f32[256,384]{0,1:T(8,128)S(1)} %slice.10), channel_id=1, source_target_pairs={{0,8},{8,0},{16,24},{24,16},{1,9},{9,1},{17,25},{25,17},{2,10},{10... | collective-permute-start | bytes 1179656 | tf_op jit(solution)/shard_map/ppermute | solution.py:33
  71.4 0.0 collective-permute-done.3
  71.4 0.0 collective-permute-done.2
  71.4 0.1 pad_maximum_fusion.1
  71.5 0.6 gather_fusion
  72.2 10.1 %all-gather.5.cloned.1.call-done = f32[1024,256]{1,0:T(8,128)} async-done(((f32[256,256]{1,0:T(8,128)}), f32[1024,256]{1,0:T(8,128)}) %all-gather.5.cloned.1.call-update) | async-done | bytes 1048592 | tf_op jit(solution)/shard_map/all_gather | solution.py:61
  82.2 5.2 %collective-permute-done = f32[256,384]{0,1:T(8,128)S(1)} collective-permute-done((f32[256,384]{0,1:T(8,128)S(1)}, f32[256,384]{0,1:T(8,128)S(1)}, u32[]{:S(2)}, u32[]{:S(2)}) %collective-permute-start) | collective-permute-done | bytes 393248 | tf_op jit(solution)/shard_map/ppermute | solution.py:33
  87.4 1.7 %convolution_add_fusion.1 = f32[256,384]{0,1:T(8,128)S(1)} fusion(f32[1024,256]{1,0:T(8,128)} %all-gather.5.cloned.1.call-done, s32[]{:T(128)S(6)} %select_n.104, f32[256,384]{0,1:T(8,128)S(1)} %collective-permute-done, pred[]{:T(512)S(6)} %eq.22, f32[4096,384]{0,1:T(8,128)} %copy-done), kind=kOutput, calls=%fused_computation.8 | convolution fusion | flops 302284800 | bytes 2229760 | tf_op jit(solution)/shard_map/dot_general | solution.py:37
  89.1 1.1 fusion.4
  90.1 0.2 copy.7
  90.3 1.1 fusion.12
  91.4 2.5 %collective-permute-start.4 = (f32[256,384]{0,1:T(8,128)S(1)}, f32[256,384]{0,1:T(8,128)S(1)}, u32[]{:S(2)}, u32[]{:S(2)}) collective-permute-start(f32[256,384]{0,1:T(8,128)S(1)} %fusion.12), channel_id=1, source_target_pairs={{0,16},{8,24},{16,0},{24,8},{1,17},{9,25},{17,1},{25,9},{2,18},{10... | collective-permute-start | bytes 1179656 | tf_op jit(solution)/shard_map/ppermute | solution.py:33
  93.9 0.0 copy-start.3
  93.9 5.7 %slice.11 = f32[3840,384]{0,1:T(8,128)} slice(f32[4096,384]{0,1:T(8,128)} %copy-done), slice={[256:4096], [0:384]} | slice | bytes 11796480 | tf_op jit(solution)/shard_map/slice | solution.py:57
  99.5 0.0 copy-done.3
  99.5 1.8 %fusion = f32[256,384]{0,1:T(8,128)S(1)} fusion(f32[256,384]{1,0:T(8,128)S(1)} %fusion.4, f32[1024,256]{1,0:T(8,128)S(1)} %copy-done.3, s32[]{:T(128)S(6)} %select_n.104, pred[]{:T(512)S(6)} %eq.22, f32[256,384]{0,1:T(8,128)S(1)} %collective-permute-done, f32[4096,384]{0,1:T(8,128)} %copy-done), kind=kOutput, calls=%fused_computation.4 | convolution fusion | flops 302284800 | bytes 1835013 | tf_op jit(solution)/shard_map/dot_general | solution.py:43
  101.3 10.3 %collective-permute-done.4 = f32[256,384]{0,1:T(8,128)S(1)} collective-permute-done((f32[256,384]{0,1:T(8,128)S(1)}, f32[256,384]{0,1:T(8,128)S(1)}, u32[]{:S(2)}, u32[]{:S(2)}) %collective-permute-start.4) | collective-permute-done | bytes 393248 | tf_op jit(solution)/shard_map/ppermute | solution.py:33
  111.6 0.5 convolution_add_fusion
  112.2 1.1 fusion.2
  113.2 0.2 copy.8
  113.4 1.8 %subtract_select_fusion = f32[256,384]{0,1:T(8,128)S(1)} fusion(f32[256,384]{0,1:T(8,128)S(1)} %copy.8, f32[256,384]{0,1:T(8,128)S(1)} %fusion, f32[256,384]{1,0:T(8,128)S(1)} %fusion.2, f32[1024,256]{1,0:T(8,128)} %all-gather.5.cloned.1.call-done, s32[]{:T(128)S(6)} %select_n.108, pred[]{:T(512)S(6)} %eq.23, pred[]{:T(512)S(6)} %eq.20, ...), kind=kOutput, calls=%fused_computation.10 | convolution fusion | flops 302579712 | bytes 2621447 | tf_op jit(solution)/shard_map/dot_general | solution.py:43
  115.2 6.0 %pad_maximum_fusion = f32[4096,384]{0,1:T(8,128)} fusion(f32[3840,384]{0,1:T(8,128)} %slice.11, f32[256,384]{0,1:T(8,128)S(1)} %subtract_select_fusion), kind=kLoop, calls=%fused_computation.1 | loop fusion | flops 1572864 | bytes 12582912 | tf_op jit(solution)/shard_map/concatenate | solution.py:83
  121.2 6.6 %copy.11 = f32[4096,384]{1,0:T(8,128)} copy(f32[4096,384]{0,1:T(8,128)} %pad_maximum_fusion) | data formatting | bytes 12582912 | tf_op jit(solution)/shard_map/concatenate | solution.py:83
  (3 shorter events, 0.0 us)
Async XLA Ops:
  6.5 43.8 %all-gather.3.cloned.1.call-start = ((), (), s32[]{:S(2)}) async-start(), calls=%async_computation | async-start | bytes 4718592 | tf_op jit(solution)/shard_map/all_gather | solution.py:49
  7.3 75.0 %all-gather.5.cloned.1.call-start = ((), (), s32[]{:S(2)}) async-start(), calls=%async_computation.1 | async-start | bytes 1310720 | tf_op jit(solution)/shard_map/all_gather | solution.py:61
  18.3 31.0 %collective-permute-start.1 = (f32[256,256]{1,0:T(8,128)S(1)}, f32[256,256]{1,0:T(8,128)S(1)}, u32[]{:S(2)}, u32[]{:S(2)}) collective-permute-start(f32[256,256]{1,0:T(8,128)S(1)} %all_gather.17), channel_id=1, source_target_pairs={{0,8},{8,16},{16,24},{24,0},{1,9},{9,17},{17,25},{25,1},{2,10},{10... | collective-permute-start | bytes 786440 | tf_op jit(solution)/shard_map/ppermute | solution.py:23
  19.9 51.5 %collective-permute-start.3 = (f32[256,256]{1,0:T(8,128)S(1)}, f32[256,256]{1,0:T(8,128)S(1)}, u32[]{:S(2)}, u32[]{:S(2)}) collective-permute-start(f32[256,256]{1,0:T(8,128)S(1)} %all_gather.17), channel_id=1, source_target_pairs={{8,0},{16,8},{24,16},{0,24},{9,1},{17,9},{25,17},{1,25},{10,2},{18... | collective-permute-start | bytes 786440 | tf_op jit(solution)/shard_map/ppermute | solution.py:25
  32.7 6.6 %copy-start.4 = (f32[32,256]{1,0:T(8,128)S(1)}, f32[32,256]{1,0:T(8,128)}, u32[]{:S(2)}) copy-start(f32[32,256]{1,0:T(8,128)} %param.7) | copy-start | bytes 98308
  49.3 22.2 %collective-permute-start.2 = (f32[256,256]{1,0:T(8,128)S(1)}, f32[256,256]{1,0:T(8,128)S(1)}, u32[]{:S(2)}, u32[]{:S(2)}) collective-permute-start(f32[256,256]{1,0:T(8,128)S(1)} %collective-permute-done.1), channel_id=1, source_target_pairs={{0,8},{8,16},{16,24},{24,0},{1,9},{9,17},{17,25},{25,1},{2,10},{10... | collective-permute-start | bytes 786440 | tf_op jit(solution)/shard_map/ppermute | solution.py:23
  50.3 10.7 %copy-start.1 = (f32[4096,384]{0,1:T(8,128)S(1)}, f32[4096,384]{0,1:T(8,128)}, u32[]{:S(2)}) copy-start(f32[4096,384]{0,1:T(8,128)} %copy.6) | copy-start | bytes 18874372
  50.3 10.7 %copy-start.2 = (f32[4096,256]{1,0:T(8,128)S(1)}, f32[4096,256]{1,0:T(8,128)}, u32[]{:S(2)}) copy-start(f32[4096,256]{1,0:T(8,128)} %all-gather.3.cloned.1.call-done) | copy-start | bytes 12582916
  67.1 2.7 %copy-start = (f32[4096,384]{0,1:T(8,128)}, f32[4096,384]{0,1:T(8,128)S(1)}, u32[]{:S(2)}) copy-start(f32[4096,384]{0,1:T(8,128)S(1)} %bitcast_subtract_fusion) | copy-start | bytes 18874372
  69.8 17.5 %collective-permute-start = (f32[256,384]{0,1:T(8,128)S(1)}, f32[256,384]{0,1:T(8,128)S(1)}, u32[]{:S(2)}, u32[]{:S(2)}) collective-permute-start(f32[256,384]{0,1:T(8,128)S(1)} %slice.10), channel_id=1, source_target_pairs={{0,8},{8,0},{16,24},{24,16},{1,9},{9,1},{17,25},{25,17},{2,10},{10... | collective-permute-start | bytes 1179656 | tf_op jit(solution)/shard_map/ppermute | solution.py:33
  91.4 20.3 %collective-permute-start.4 = (f32[256,384]{0,1:T(8,128)S(1)}, f32[256,384]{0,1:T(8,128)S(1)}, u32[]{:S(2)}, u32[]{:S(2)}) collective-permute-start(f32[256,384]{0,1:T(8,128)S(1)} %fusion.12), channel_id=1, source_target_pairs={{0,16},{8,24},{16,0},{24,8},{1,17},{9,25},{17,1},{25,9},{2,18},{10... | collective-permute-start | bytes 1179656 | tf_op jit(solution)/shard_map/ppermute | solution.py:33
  93.9 5.7 %copy-start.3 = (f32[1024,256]{1,0:T(8,128)S(1)}, f32[1024,256]{1,0:T(8,128)}, u32[]{:S(2)}) copy-start(f32[1024,256]{1,0:T(8,128)} %all-gather.5.cloned.1.call-done) | copy-start | bytes 3145732
Sparse Core Ops, SparseCore 0:
  9.2 41.0 all-gather.2
  51.9 30.2 all-gather.4
